TPU v7x, 512 devices: a whole 4x4x16 slice. The times are simulated.
512 devices in a mesh: seq: 64 (over z, x), ch: 8 (over y, core).
Axes of the slice: x: 4, y: 4, z: 16, core: 2. Of those that a mesh axis runs over, the one named last changes fastest.
Arguments:
- signal: float32 [16384, 4096], P('seq', 'ch'), may hold values from -6 to 6
- filters: float32 [16384, 256], P(('seq', 'ch')), may hold values from -1 to 1
- skip_gain: float32 [4096], P('ch'), may hold values from -1 to 1
Outputs:
- filtered: float32 [16384, 4096], P('seq', 'ch')
All inputs are finite; a program needn't handle non-finite values.
Results may differ from a plain program's by a relative error of at most 0.00009.
Values sent between devices are 32-bit elements; how exact they have to be, the bound alone decides.
A program may use at most 64 MiB of HBM per device.

v0:
```python
import math

import jax
import jax.numpy as jnp
from jax import lax
from jax.sharding import PartitionSpec as P

GROUP = 16


HIGHEST_PRECISION = lax.Precision.HIGHEST


def angle_table(row_count, col_count, length, sign):
    row_index = jnp.arange(row_count, dtype=jnp.int32)[:, None]
    col_index = jnp.arange(col_count, dtype=jnp.int32)[None, :]
    phase = row_index * col_index % length
    angle = sign * 2.0 * math.pi / length * phase.astype(jnp.float32)
    return (jnp.cos(angle), jnp.sin(angle))


def complex_apply(form, table, real_part, imag_part):
    cosine, sine = table

    def product(matrix, values):
        return jnp.einsum(form, matrix, values, precision=HIGHEST_PRECISION)

    if imag_part is None:
        return (product(cosine, real_part), product(sine, real_part))
    return (
        product(cosine, real_part) - product(sine, imag_part),
        product(cosine, imag_part) + product(sine, real_part),
    )


def rotate(real_part, imag_part, cosine, sine):
    return (real_part * cosine - imag_part * sine, real_part * sine + imag_part * cosine)


def local_convolve(whole_sig, whole_taps, blocks, rows):
    width = whole_sig.shape[1]
    span = 2 * blocks * rows
    sig_blocks = whole_sig.reshape(blocks, rows, width)
    tap_blocks = whole_taps.reshape(blocks, rows, width)
    outer = angle_table(2 * blocks, blocks, 2 * blocks, -1.0)
    sig_real, sig_imag = complex_apply("kn,nbc->kbc", outer, sig_blocks, None)
    filt_real, filt_imag = complex_apply("kn,nbc->kbc", outer, tap_blocks, None)
    phase = (
        jnp.arange(2 * blocks, dtype=jnp.int32)[:, None]
        * jnp.arange(rows, dtype=jnp.int32)[None, :]
        % span
    )
    twist = 2.0 * math.pi / span * phase.astype(jnp.float32)
    twist_cos = jnp.cos(twist)[:, :, None]
    twist_sin = jnp.sin(twist)[:, :, None]
    sig_real, sig_imag = rotate(sig_real, sig_imag, twist_cos, -twist_sin)
    filt_real, filt_imag = rotate(filt_real, filt_imag, twist_cos, -twist_sin)
    inner = angle_table(rows, rows, rows, -1.0)
    sig_real, sig_imag = complex_apply("kn,bnc->bkc", inner, sig_real, sig_imag)
    filt_real, filt_imag = complex_apply("kn,bnc->bkc", inner, filt_real, filt_imag)
    prod_real, prod_imag = rotate(sig_real, sig_imag, filt_real, filt_imag)
    inverse_inner = angle_table(rows, rows, rows, 1.0)
    back_real, back_imag = complex_apply("nk,bkc->bnc", inverse_inner, prod_real, prod_imag)
    back_real, back_imag = rotate(back_real, back_imag, twist_cos, twist_sin)
    outer_back = angle_table(blocks, 2 * blocks, 2 * blocks, 1.0)
    values = jnp.einsum(
        "nk,kbc->nbc", outer_back[0], back_real, precision=HIGHEST_PRECISION
    ) - jnp.einsum("nk,kbc->nbc", outer_back[1], back_imag, precision=HIGHEST_PRECISION)
    return values.reshape(blocks * rows, width) / span


def body(signal, filters, skip_gain):
    blocks = lax.axis_size("seq")
    rows = signal.shape[0]
    taps = lax.all_to_all(filters, "ch", split_axis=1, concat_axis=0, tiled=True)
    local_groups = taps.shape[1]
    per_channel = jnp.broadcast_to(taps[:, :, None], (rows, local_groups, GROUP)).reshape(
        rows, local_groups * GROUP
    )
    whole_sig, whole_taps = (
        lax.all_to_all(signal, "seq", split_axis=1, concat_axis=0, tiled=True),
        lax.all_to_all(per_channel, "seq", split_axis=1, concat_axis=0, tiled=True),
    )
    values = local_convolve(whole_sig, whole_taps, blocks, rows)
    homed = lax.all_to_all(values, "seq", split_axis=0, concat_axis=1, tiled=True)
    return homed + skip_gain[None, :] * signal


def solution(mesh):
    placed = (P("seq", "ch"), P(("seq", "ch"), None), P("ch"))
    return jax.shard_map(
        body, mesh=mesh, in_specs=placed, out_specs=P("seq", "ch"), check_vma=False
    )
```

profile of v0, /device:TPU:2, one launch (start us, length us, event | category | flops | bytes accessed | tf_op | source)
XLA Modules:
  0.0 164.8 jit_solution(10516837235378712550)
XLA Ops:
  0.0 0.9 copy.12
  0.9 0.7 reshape.78
  1.6 4.5 %all-to-all-start.1 = ((f32[8,1,1024]{2,1,0:T(1,128)}), f32[8,1,1024]{2,1,0:T(1,128)S(1)}, u32[]{:S(2)}, u32[]{:S(2)}) async-start(f32[8,1,1024]{2,1,0:T(1,128)} %reshape.78), calls=%async_computation.1 | async-start | bytes 65536 | tf_op jit(solution)/shard_map/all_to_all | solution.py:75
  6.1 2.1 %copy.10 = f32[256,512]{0,1:T(8,128)} copy(f32[256,512]{1,0:T(8,128)} %param.3) | data formatting | bytes 1048576 | tf_op args[0]
  8.1 3.4 %all-to-all-done.1 = f32[8,1,1024]{2,1,0:T(1,128)S(1)} async-done(((f32[8,1,1024]{2,1,0:T(1,128)}), f32[8,1,1024]{2,1,0:T(1,128)S(1)}, u32[]{:S(2)}, u32[]{:S(2)}) %all-to-all-start.1) | async-done | bytes 32800 | tf_op jit(solution)/shard_map/all_to_all | solution.py:75
  11.5 18.6 %all-to-all-start = ((f32[256,64,8]{0,2,1:T(8,128)}), f32[256,64,8]{0,2,1:T(8,128)S(1)}, u32[]{:S(2)}, u32[]{:S(2)}) async-start(f32[256,64,8]{0,2,1:T(8,128)} %bitcast.2), calls=%async_computation | async-start | bytes 1048576 | tf_op jit(solution)/shard_map/all_to_all | solution.py:81
  30.2 0.5 broadcast.180
  30.7 0.7 reduce
  31.4 0.1 reshape.79
  31.5 0.1 copy.13
  31.6 0.1 broadcast_in_dim.8
  31.8 31.0 %all-to-all-done = f32[256,64,8]{0,2,1:T(8,128)S(1)} async-done(((f32[256,64,8]{0,2,1:T(8,128)}), f32[256,64,8]{0,2,1:T(8,128)S(1)}, u32[]{:S(2)}, u32[]{:S(2)}) %all-to-all-start) | async-done | bytes 524320 | tf_op jit(solution)/shard_map/all_to_all | solution.py:81
  62.8 0.8 broadcast_in_dim.11
  63.6 6.4 %all-to-all-start.2 = ((f32[256,64,8]{0,2,1:T(8,128)}), f32[256,64,8]{0,2,1:T(8,128)S(1)}, u32[]{:S(2)}, u32[]{:S(2)}) async-start(f32[256,64,8]{0,2,1:T(8,128)} %broadcast_in_dim.11), calls=%async_computation.2 | async-start | bytes 1048576 | tf_op jit(solution)/shard_map/all_to_all | solution.py:82
  70.1 0.5 fusion.83
  70.6 0.5 fusion.84
  71.1 1.2 fusion.20
  72.3 1.2 fusion.22
  73.5 3.0 %fusion.44 = f32[128,8,256]{2,0,1:T(8,128)} fusion(f32[128,256,8]{1,0,2:T(8,128)S(1)} %fusion.20, f32[128,256,8]{1,0,2:T(8,128)S(1)} %fusion.22, f32[128,256]{1,0:T(8,128)S(1)} %get-tuple-element.8, f32[128,256]{1,0:T(8,128)S(1)} %get-tuple-element.7), kind=kOutput, calls=%fused_computation.61 | convolution fusion | flops 807010304 | bytes 3407872 | tf_op jit(solution)/shard_map/kn,bnc->bkc/dot_general | solution.py:26
  76.4 2.0 %fusion.48 = f32[128,8,256]{2,0,1:T(8,128)S(1)} fusion(f32[128,256,8]{1,0,2:T(8,128)S(1)} %fusion.20, f32[128,256,8]{1,0,2:T(8,128)S(1)} %fusion.22, f32[128,256]{1,0:T(8,128)S(1)} %get-tuple-element.8, f32[128,256]{1,0:T(8,128)S(1)} %get-tuple-element.7), kind=kOutput, calls=%fused_computation.65 | convolution fusion | flops 807010304 | bytes 3407872 | tf_op jit(solution)/shard_map/kn,bnc->bkc/dot_general | solution.py:26
  78.4 3.0 %convolution_subtract_fusion.2 = f32[128,8,256]{2,0,1:T(8,128)} fusion(f32[128,8,256]{2,0,1:T(8,128)S(1)} %fusion.48, f32[128,256,8]{1,0,2:T(8,128)S(1)} %fusion.20, f32[128,256,8]{1,0,2:T(8,128)S(1)} %fusion.22, f32[128,256]{1,0:T(8,128)S(1)} %get-tuple-element.8, f32[128,256]{1,0:T(8,128)S(1)} %get-tuple-element.7), kind=kOutput, calls=%fused_computation.5 | convolution fusion | flops 807272448 | bytes 4456448 | tf_op jit(solution)/shard_map/kn,bnc->bkc/dot_general | solution.py:26
  81.4 20.1 %all-to-all-done.2 = f32[256,64,8]{0,2,1:T(8,128)S(1)} async-done(((f32[256,64,8]{0,2,1:T(8,128)}), f32[256,64,8]{0,2,1:T(8,128)S(1)}, u32[]{:S(2)}, u32[]{:S(2)}) %all-to-all-start.2) | async-done | bytes 524320 | tf_op jit(solution)/shard_map/all_to_all | solution.py:82
  101.5 1.2 fusion.16
  102.7 1.4 fusion.18
  104.1 2.0 %fusion.42 = f32[128,8,256]{2,0,1:T(8,128)S(1)} fusion(f32[128,256,8]{1,0,2:T(8,128)S(1)} %fusion.16, f32[128,256,8]{1,0,2:T(8,128)S(1)} %fusion.18, f32[128,256]{1,0:T(8,128)S(1)} %get-tuple-element.8, f32[128,256]{1,0:T(8,128)S(1)} %get-tuple-element.7), kind=kOutput, calls=%fused_computation.59 | convolution fusion | flops 807010304 | bytes 3407872 | tf_op jit(solution)/shard_map/kn,bnc->bkc/dot_general | solution.py:26
  106.1 2.0 %fusion.46 = f32[128,8,256]{2,0,1:T(8,128)S(1)} fusion(f32[128,256,8]{1,0,2:T(8,128)S(1)} %fusion.16, f32[128,256,8]{1,0,2:T(8,128)S(1)} %fusion.18, f32[128,256]{1,0:T(8,128)S(1)} %get-tuple-element.8, f32[128,256]{1,0:T(8,128)S(1)} %get-tuple-element.7), kind=kOutput, calls=%fused_computation.63 | convolution fusion | flops 807010304 | bytes 3407872 | tf_op jit(solution)/shard_map/kn,bnc->bkc/dot_general | solution.py:26
  108.1 2.0 %convolution_add_fusion.1 = f32[128,8,256]{2,0,1:T(8,128)S(1)} fusion(f32[128,8,256]{2,0,1:T(8,128)S(1)} %fusion.42, f32[128,256,8]{1,0,2:T(8,128)S(1)} %fusion.16, f32[128,256,8]{1,0,2:T(8,128)S(1)} %fusion.18, f32[128,256]{1,0:T(8,128)S(1)} %get-tuple-element.8, f32[128,256]{1,0:T(8,128)S(1)} %get-tuple-element.7), kind=kOutput, calls=%fused_computation.2 | convolution fusion | flops 807272448 | bytes 4456448 | tf_op jit(solution)/shard_map/kn,bnc->bkc/dot_general | solution.py:26
  110.1 0.0 copy-start
  110.1 0.0 copy-start.1
  110.1 2.0 %convolution_subtract_fusion.1 = f32[128,8,256]{2,0,1:T(8,128)S(1)} fusion(f32[128,8,256]{2,0,1:T(8,128)S(1)} %fusion.46, f32[128,256,8]{1,0,2:T(8,128)S(1)} %fusion.16, f32[128,256,8]{1,0,2:T(8,128)S(1)} %fusion.18, f32[128,256]{1,0:T(8,128)S(1)} %get-tuple-element.8, f32[128,256]{1,0:T(8,128)S(1)} %get-tuple-element.7), kind=kOutput, calls=%fused_computation.4 | convolution fusion | flops 807272448 | bytes 4456448 | tf_op jit(solution)/shard_map/kn,bnc->bkc/dot_general | solution.py:26
  112.1 0.0 copy-done
  112.1 0.0 copy-done.1
  112.2 2.2 %multiply_subtract_fusion = (f32[128,8,256]{2,0,1:T(8,128)S(1)}, f32[128,8,256]{2,0,1:T(8,128)S(1)}) fusion(f32[128,8,256]{2,0,1:T(8,128)S(1)} %convolution_add_fusion.1, f32[128,8,256]{2,0,1:T(8,128)S(1)} %copy-done, f32[128,8,256]{2,0,1:T(8,128)S(1)} %convolution_subtract_fusion.1, f32[128,8,256]{2,0,1:T(8,128)S(1)} %copy-done.1, ...), kind=kOutput, calls=%fused_computation.24 | convolution fusion | flops 808845312 | bytes 8650752 | tf_op jit(solution)/shard_map/kn,bnc->bkc/dot_general | solution.py:26
  114.4 2.2 %fusion.8 = f32[128,8,256]{2,0,1:T(8,128)S(1)} fusion(f32[128,8,256]{2,0,1:T(8,128)S(1)} %get-tuple-element.5), kind=kOutput, calls=%fused_computation.15 | convolution fusion | flops 806223872 | bytes 2097152 | tf_op jit(solution)/shard_map/nk,bkc->bnc/dot_general | solution.py:26
  116.6 2.0 %fusion.4 = f32[128,8,256]{2,0,1:T(8,128)S(1)} fusion(f32[128,8,256]{2,0,1:T(8,128)S(1)} %get-tuple-element.6), kind=kOutput, calls=%fused_computation.11 | convolution fusion | flops 806223872 | bytes 2097152 | tf_op jit(solution)/shard_map/nk,bkc->bnc/dot_general | solution.py:26
  118.5 2.0 %convolution_subtract_fusion = f32[128,8,256]{2,0,1:T(8,128)S(1)} fusion(f32[128,8,256]{2,0,1:T(8,128)S(1)} %fusion.8, f32[128,8,256]{2,0,1:T(8,128)S(1)} %get-tuple-element.6), kind=kOutput, calls=%fused_computation.1 | convolution fusion | flops 806486016 | bytes 3145728 | tf_op jit(solution)/shard_map/nk,bkc->bnc/dot_general | solution.py:26
  120.5 2.0 %convolution_add_fusion = f32[128,8,256]{2,0,1:T(8,128)S(1)} fusion(f32[128,8,256]{2,0,1:T(8,128)S(1)} %fusion.4, f32[128,8,256]{2,0,1:T(8,128)S(1)} %get-tuple-element.5), kind=kOutput, calls=%fused_computation | convolution fusion | flops 806486016 | bytes 3145728 | tf_op jit(solution)/shard_map/nk,bkc->bnc/dot_general | solution.py:26
  122.5 0.9 fusion.2
  123.4 0.9 fusion
  124.4 0.3 copy.15
  124.7 0.0 copy-start.2
  124.7 37.7 %all_to_all.61 = f32[64,256,8]{1,2,0:T(8,128)S(1)} all-to-all(f32[64,256,8]{1,2,0:T(8,128)S(1)} %copy.15), channel_id=1, replica_groups=mesh['seq'=64,'ch'=8] {'seq'}, dimensions={0} | all-to-all | bytes 1048576 | tf_op jit(solution)/shard_map/all_to_all | solution.py:85
  162.4 0.0 copy-done.2
  162.4 1.2 bitcast_add_fusion
  163.6 1.0 copy.17
  (3 shorter events, 0.1 us)
Async XLA Ops:
  1.6 9.9 %all-to-all-start.1 = ((f32[8,1,1024]{2,1,0:T(1,128)}), f32[8,1,1024]{2,1,0:T(1,128)S(1)}, u32[]{:S(2)}, u32[]{:S(2)}) async-start(f32[8,1,1024]{2,1,0:T(1,128)} %reshape.78), calls=%async_computation.1 | async-start | bytes 65536 | tf_op jit(solution)/shard_map/all_to_all | solution.py:75
  11.5 51.3 %all-to-all-start = ((f32[256,64,8]{0,2,1:T(8,128)}), f32[256,64,8]{0,2,1:T(8,128)S(1)}, u32[]{:S(2)}, u32[]{:S(2)}) async-start(f32[256,64,8]{0,2,1:T(8,128)} %bitcast.2), calls=%async_computation | async-start | bytes 1048576 | tf_op jit(solution)/shard_map/all_to_all | solution.py:81
  63.6 37.9 %all-to-all-start.2 = ((f32[256,64,8]{0,2,1:T(8,128)}), f32[256,64,8]{0,2,1:T(8,128)S(1)}, u32[]{:S(2)}, u32[]{:S(2)}) async-start(f32[256,64,8]{0,2,1:T(8,128)} %broadcast_in_dim.11), calls=%async_computation.2 | async-start | bytes 1048576 | tf_op jit(solution)/shard_map/all_to_all | solution.py:82
  110.1 2.0 %copy-start = (f32[128,8,256]{2,0,1:T(8,128)S(1)}, f32[128,8,256]{2,0,1:T(8,128)}, u32[]{:S(2)}) copy-start(f32[128,8,256]{2,0,1:T(8,128)} %convolution_subtract_fusion.2) | copy-start | bytes 3145732
  110.1 2.0 %copy-start.1 = (f32[128,8,256]{2,0,1:T(8,128)S(1)}, f32[128,8,256]{2,0,1:T(8,128)}, u32[]{:S(2)}) copy-start(f32[128,8,256]{2,0,1:T(8,128)} %fusion.44) | copy-start | bytes 3145732
  124.7 37.7 %copy-start.2 = (f32[512]{0:T(512)S(1)}, f32[512]{0:T(512)}, u32[]{:S(2)}) copy-start(f32[512]{0:T(512)} %param.5) | copy-start | bytes 6148
where the time goes:
time: 168 us; the launch traced here: 165 us
  waiting for transfers between devices  54.5 us (32%)
  blocking collectives  37.7 us (22%)
  matrix products  33 us (20%)
  starting transfers between devices  29.5 us (18%)
  local copies, waits for them, and re-layouts  6.66 us (4%)
  other arithmetic  2.92 us (2%)
    all_to_all x1, blocking collectives, body(): lax.all_to_all(values, 'seq', split_axis=0, concat_axis=1, tiled=True)  37.7 us
    dot_general x16, matrix products, product(): return jnp.einsum(form, matrix, values, precision=HIGHEST_PRECISION)  31.2 us
    all_to_all x1, waiting for transfers between devices, body(): lax.all_to_all(signal, 'seq', split_axis=1, concat_axis=0, tiled=True)  31 us
    all_to_all x1, waiting for transfers between devices, body(): lax.all_to_all(per_channel, 'seq', split_axis=1, concat_axis=0, tiled=True)  20.1 us
    all_to_all x1, starting transfers between devices, body(): lax.all_to_all(signal, 'seq', split_axis=1, concat_axis=0, tiled=True)  18.6 us
    all_to_all x1, starting transfers between devices, body(): lax.all_to_all(per_channel, 'seq', split_axis=1, concat_axis=0, tiled=True)  6.42 us
    all_to_all x1, starting transfers between devices, body(): lax.all_to_all(filters, 'ch', split_axis=1, concat_axis=0, tiled=True)  4.47 us
    unnamed x10, local copies, waits for them, and re-layouts  3.75 us
  transfers between devices with their start and end apart: 3, of which 3 were waited for; matrix products, arithmetic and copies ran while one was open for 9% of the time, Pallas kernels for 0%

commit v1 on v0

v1 whole, which is shorter than its diff:
```python
import functools

import jax
import jax.numpy as jnp
from jax import lax
from jax.experimental import pallas as pl
from jax.experimental.pallas import tpu as pltpu
from jax.sharding import PartitionSpec as P

GROUP = 16
LANES = 128
MESH = pl.DeviceIdType.MESH
BF = jnp.bfloat16
F32 = jnp.float32


def split(value):
    high = value.astype(BF)
    return high, (value - high.astype(F32)).astype(BF)


def exchange_kernel(
    n, sig_ref, tap_ref, out_ref, xbuf, hbuf, ybuf, xx_hi, xx_lo, strip_hi, strip_lo,
    tap_out, sig_out, out_out, tap_sem, sig_sem, out_sem,
):
    me = lax.axis_index("seq")
    cpd, rows = sig_ref.shape[1], sig_ref.shape[2]
    per = rows // LANES
    barrier = pltpu.get_barrier_semaphore()

    def peer(step):
        return lax.rem(me + step, n)

    @pl.loop(1, n)
    def _(step):
        pl.semaphore_signal(barrier, inc=1, device_id={"seq": peer(step)}, device_id_type=MESH)

    pl.semaphore_wait(barrier, n - 1)

    def tap_copy(step):
        other = peer(step)
        return pltpu.make_async_remote_copy(
            src_ref=tap_ref.at[other // 2], dst_ref=hbuf.at[me + 1], send_sem=tap_out,
            recv_sem=tap_sem, device_id={"seq": other}, device_id_type=MESH,
        )

    def sig_copy(step):
        other = peer(step)
        return pltpu.make_async_remote_copy(
            src_ref=sig_ref.at[other], dst_ref=xbuf.at[me], send_sem=sig_out,
            recv_sem=sig_sem, device_id={"seq": other}, device_id_type=MESH,
        )

    def out_copy(step):
        other = peer(step)
        return pltpu.make_async_remote_copy(
            src_ref=ybuf.at[other], dst_ref=out_ref.at[me], send_sem=out_out,
            recv_sem=out_sem, device_id={"seq": other}, device_id_type=MESH,
        )

    @pl.loop(1, n)
    def _(step):
        tap_copy(step).start()

    @pl.loop(1, n)
    def _(step):
        sig_copy(step).start()

    hbuf[0] = jnp.zeros((1, rows), F32)
    hbuf[me + 1] = tap_ref[me // 2]
    xbuf[me] = sig_ref[me]

    def wait_all(ref, sem):
        whole = ref.at[pl.ds(0, n - 1)]
        pltpu.make_async_copy(whole, whole, sem).wait()

    wait_all(hbuf, tap_sem)

    strip_hi[0] = jnp.zeros((LANES, LANES), BF)
    strip_lo[0] = jnp.zeros((LANES, LANES), BF)

    def build(pair, block):
        spread = jnp.broadcast_to(pair, (LANES, 2 * LANES))
        rolled = pltpu.roll(spread, 0, 1, stride=1, stride_axis=0)[:, LANES:]
        high, low = split(rolled)
        strip_hi[block] = high
        strip_lo[block] = low

    @pl.loop(0, n)
    def _(source):
        before = hbuf[source, :, rows - LANES:]
        build(jnp.concatenate([before, hbuf[source + 1, :, :LANES]], axis=1), source * per + 1)
        for part in range(1, per):
            pair = hbuf[source + 1, :, (part - 1) * LANES:(part + 1) * LANES]
            build(pair, source * per + part + 1)

    wait_all(xbuf, sig_sem)

    total = n * cpd
    pad = xx_hi.shape[0] - total
    high, low = split(xbuf[...].reshape(total, rows))
    zero = jnp.zeros((pad, 2 * rows), BF)
    for where, value in ((xx_hi, high), (xx_lo, low)):
        where[:pad] = zero
        where[pad:, :rows] = value
        where[pad:, rows:] = jnp.concatenate([jnp.zeros((cpd, rows), BF), value[:-cpd]], axis=0)

    def toeplitz(strip, step):
        first = step * 2 * per

        def line(start):
            return jnp.concatenate([strip[start + part] for part in range(per)], axis=1)

        lines = []
        for lag in range(2):
            for part in range(per):
                lines.append(line(first + lag * per + 1 - part))
        return jnp.concatenate(lines, axis=0)

    inner = pad // (2 * cpd) + 1
    buckets = n // (2 * inner)
    for bucket in range(buckets):
        base = bucket * inner * 2 * cpd
        height = total - base
        owner = pl.ds(base // cpd, height // cpd)

        def product(offset, bucket=bucket, height=height):
            step = bucket * inner + offset
            window = pl.ds(pl.multiple_of(pad - 2 * cpd * offset, 2 * cpd), height)
            weight_hi, weight_lo = toeplitz(strip_hi, step), toeplitz(strip_lo, step)
            lhs_hi, lhs_lo = xx_hi[window, :], xx_lo[window, :]
            dot = functools.partial(jnp.dot, preferred_element_type=F32)
            value = dot(lhs_hi, weight_hi) + dot(lhs_lo, weight_hi) + dot(lhs_hi, weight_lo)
            return value.reshape(height // cpd, cpd, rows)

        if bucket == 0:
            ybuf[...] = product(0)
            first = 1
        else:
            first = 0

        @pl.loop(first, inner)
        def _(offset, owner=owner, product=product):
            ybuf[owner] += product(offset)

    @pl.loop(1, n)
    def _(step):
        out_copy(step).start()

    out_ref[me] = ybuf[me]

    wait_all(out_ref, out_sem)
    wait_all(hbuf, tap_out)
    wait_all(xbuf, sig_out)
    wait_all(ybuf, out_out)


def exchange(sig, taps):
    n, cpd, rows = sig.shape
    total, pad = n * cpd, 6 * cpd
    blocks = n * rows // LANES + 1
    vmem = pl.BlockSpec(memory_space=pltpu.VMEM)
    return pl.pallas_call(
        functools.partial(exchange_kernel, n),
        out_shape=jax.ShapeDtypeStruct(sig.shape, F32),
        in_specs=[vmem, vmem],
        out_specs=vmem,
        scratch_shapes=[
            pltpu.VMEM(sig.shape, F32),
            pltpu.VMEM((n + 1, 1, rows), F32),
            pltpu.VMEM(sig.shape, F32),
            pltpu.VMEM((pad + total, 2 * rows), BF),
            pltpu.VMEM((pad + total, 2 * rows), BF),
            pltpu.VMEM((blocks, LANES, LANES), BF),
            pltpu.VMEM((blocks, LANES, LANES), BF),
            *[pltpu.SemaphoreType.DMA] * 6,
        ],
        compiler_params=pltpu.CompilerParams(
            collective_id=0, has_side_effects=True, vmem_limit_bytes=48 * 1024 * 1024
        ),
    )(sig, taps)


def body(signal, filters, skip_gain):
    n = lax.axis_size("seq")
    rows, width = signal.shape
    taps = lax.all_to_all(filters, "ch", split_axis=1, concat_axis=0, tiled=True)
    groups = taps.shape[1]
    taps = taps.T.reshape(groups, 1, rows)
    sig = signal.T.reshape(n, width // n, rows)
    values = exchange(sig, taps)
    return values.reshape(width, rows).T + skip_gain[None, :] * signal


def solution(mesh):
    placed = (P("seq", "ch"), P(("seq", "ch"), None), P("ch"))
    return jax.shard_map(
        body, mesh=mesh, in_specs=placed, out_specs=P("seq", "ch"), check_vma=False
    )
```

time: 168 us -> 99.3 us (0.59)
  the two profiles are of different devices: /device:TPU:2 before, /device:TPU:1 now
where the time goes in v1:
time: 99.3 us; the launch traced here: 99 us
  Pallas kernels  79 us (80%)
  starting transfers between devices  10.1 us (10%)
  local copies, waits for them, and re-layouts  4.66 us (5%)
  waiting for transfers between devices  3.49 us (4%)
  other arithmetic  1.61 us (2%)
    pallas_call x1, Pallas kernels, exchange(): pl.pallas_call(functools.partial(exchange_kernel, n), out_shape=jax.Shape...  79 us
    all_to_all x1, starting transfers between devices, body(): lax.all_to_all(filters, 'ch', split_axis=1, concat_axis=0, tiled=True)  10.1 us
    all_to_all x1, waiting for transfers between devices, body(): lax.all_to_all(filters, 'ch', split_axis=1, concat_axis=0, tiled=True)  3.49 us
    unnamed x7, local copies, waits for them, and re-layouts  2.51 us
  transfers between devices with their start and end apart: 1, of which 1 were waited for; matrix products, arithmetic and copies ran while one was open for 1% of the time, Pallas kernels for 0%

profile of v1, /device:TPU:1, one launch (start us, length us, event | category | flops | bytes accessed | tf_op | source)
XLA Modules:
  0.0 99.0 jit_solution(15936994317270068729)
XLA Ops:
  0.0 0.9 copy.8
  0.9 0.7 reshape.16
  1.6 10.1 %all-to-all-start = ((f32[8,1,1024]{2,1,0:T(1,128)}), f32[8,1,1024]{2,1,0:T(1,128)S(1)}, u32[]{:S(2)}, u32[]{:S(2)}) async-start(f32[8,1,1024]{2,1,0:T(1,128)} %reshape.16), calls=%async_computation | async-start | bytes 65536 | tf_op jit(solution)/shard_map/all_to_all | solution.py:187
  11.7 1.2 %copy.7 = f32[512,256]{1,0:T(8,128)S(1)} copy(f32[512,256]{0,1:T(8,128)} %bitcast.16) | data formatting | bytes 1048576 | tf_op jit(solution)/shard_map/transpose | solution.py:190
  13.0 3.5 %all-to-all-done = f32[8,1,1024]{2,1,0:T(1,128)S(1)} async-done(((f32[8,1,1024]{2,1,0:T(1,128)}), f32[8,1,1024]{2,1,0:T(1,128)S(1)}, u32[]{:S(2)}, u32[]{:S(2)}) %all-to-all-start) | async-done | bytes 32800 | tf_op jit(solution)/shard_map/all_to_all | solution.py:187
  16.5 0.5 broadcast.1
  17.0 0.7 reduce
  17.7 0.1 reshape.17
  17.8 0.1 copy.9
  17.9 0.1 all_to_all.17
  18.0 79.0 %shard_map.37 = f32[64,8,256]{2,1,0:T(8,128)S(1)} custom-call(f32[64,8,256]{2,1,0:T(8,128)S(1)} %bitcast.14, f32[32,1,256]{2,1,0:T(1,128)S(1)} %reshape.14.tap_ref), custom_call_target="tpu_custom_call" | custom-call | tf_op jit(solution)/shard_map/pallas_call | solution.py:163
  97.0 0.0 copy-start
  97.1 0.0 copy-start.1
  97.1 0.2 copy.10
  97.3 0.8 copy-done
  98.1 0.0 copy-done.1
  98.1 0.9 bitcast_add_fusion
  (2 shorter events, 0.0 us)
Async XLA Ops:
  1.6 14.9 %all-to-all-start = ((f32[8,1,1024]{2,1,0:T(1,128)}), f32[8,1,1024]{2,1,0:T(1,128)S(1)}, u32[]{:S(2)}, u32[]{:S(2)}) async-start(f32[8,1,1024]{2,1,0:T(1,128)} %reshape.16), calls=%async_computation | async-start | bytes 65536 | tf_op jit(solution)/shard_map/all_to_all | solution.py:187
  97.0 1.0 %copy-start = (f32[256,512]{1,0:T(8,128)S(1)}, f32[256,512]{1,0:T(8,128)}, u32[]{:S(2)}) copy-start(f32[256,512]{1,0:T(8,128)} %param.3) | copy-start | bytes 1572868
  97.1 1.0 %copy-start.1 = (f32[512]{0:T(512)S(1)}, f32[512]{0:T(512)}, u32[]{:S(2)}) copy-start(f32[512]{0:T(512)} %param.5) | copy-start | bytes 6148

commit v2 on v1

--- a/solution.py
+++ b/solution.py
@@ -20,22 +20,47 @@
 
 
 def exchange_kernel(
-    n, sig_ref, tap_ref, out_ref, xbuf, hbuf, ybuf, xx_hi, xx_lo, strip_hi, strip_lo,
-    tap_out, sig_out, out_out, tap_sem, sig_sem, out_sem,
+    n, m, sig_in, tap_in, out_ref, sig_ref, part_out, part_in, tap_ref, xbuf, hbuf, ybuf, xx_hi, xx_lo,
+    strip_hi, strip_lo, part_send, tap_out, sig_out, out_out, part_sem, tap_sem, sig_sem, out_sem,
 ):
     me = lax.axis_index("seq")
+    mine = lax.axis_index("ch")
     cpd, rows = sig_ref.shape[1], sig_ref.shape[2]
     per = rows // LANES
     barrier = pltpu.get_barrier_semaphore()
 
     def peer(step):
-        return lax.rem(me + step, n)
+        away = n // 2 - step // 2
+        return lax.rem(me + jnp.where(step % 2 == 1, away, n - away), n)
 
     @pl.loop(1, n)
     def _(step):
         pl.semaphore_signal(barrier, inc=1, device_id={"seq": peer(step)}, device_id_type=MESH)
 
-    pl.semaphore_wait(barrier, n - 1)
+    @pl.loop(1, m)
+    def _(step):
+        pl.semaphore_signal(barrier, inc=1, device_id={"ch": lax.rem(mine + step, m)}, device_id_type=MESH)
+
+    lags = tap_in.shape[0]
+    slots = LANES // lags
+    tiled = jnp.concatenate([tap_in[...]] * slots, axis=0).T
+    lane = lax.broadcasted_iota(jnp.int32, tiled.shape, 1)
+    start = lags * lax.rem(mine, slots)
+    tiled = jnp.where((lane >= start) & (lane < start + lags), tiled, 0.0)
+    part_out[...] = tiled.reshape(part_out.shape)
+
+    for first in range(0, n * cpd, LANES):
+        turned = sig_in[:, first:first + LANES].T
+        sig_ref[first // cpd:(first + LANES) // cpd] = turned.reshape(LANES // cpd, cpd, rows)
+
+    pl.semaphore_wait(barrier, n + m - 2)
+
+    def part_copy(step):
+        other = lax.rem(mine + step, m)
+        return pltpu.make_async_remote_copy(
+            src_ref=part_out.at[other], dst_ref=part_in.at[mine], send_sem=part_send,
+            recv_sem=part_sem, device_id={"ch": other}, device_id_type=MESH,
+        )
 
     def tap_copy(step):
         other = peer(step)
@@ -52,17 +77,41 @@
         )
 
     def out_copy(step):
-        other = peer(step)
+        other = step
         return pltpu.make_async_remote_copy(
             src_ref=ybuf.at[other], dst_ref=out_ref.at[me], send_sem=out_out,
             recv_sem=out_sem, device_id={"seq": other}, device_id_type=MESH,
         )
 
+    @pl.loop(1, m)
+    def _(step):
+        part_copy(step).start()
+
+    ahead = n // 4
+
+    @pl.loop(1, ahead)
+    def _(step):
+        sig_copy(step).start()
+
+    part_in[mine] = part_out[mine]
+    whole = part_in.at[pl.ds(0, m - 1)]
+    pltpu.make_async_copy(whole, whole, part_sem).wait()
+    for half in range(m // slots):
+        value = part_in[half * slots]
+        for slot in range(1, slots):
+            value = value + part_in[half * slots + slot]
+        for group in range(n // 2):
+            tap_ref[group, :, half * LANES:(half + 1) * LANES] = value[group:group + 1]
+
+    @pl.loop(ahead, ahead + 4)
+    def _(step):
+        sig_copy(step).start()
+
     @pl.loop(1, n)
     def _(step):
         tap_copy(step).start()
 
-    @pl.loop(1, n)
+    @pl.loop(ahead + 4, n)
     def _(step):
         sig_copy(step).start()
 
@@ -143,52 +192,61 @@
         def _(offset, owner=owner, product=product):
             ybuf[owner] += product(offset)
 
-    @pl.loop(1, n)
-    def _(step):
-        out_copy(step).start()
+        span = 2 * inner
+
+        @pl.loop(0, span)
+        def _(turn, bucket=bucket):
+            other = bucket * span + lax.rem(me + turn, span)
+
+            @pl.when(other != me)
+            def _():
+                out_copy(other).start()
 
     out_ref[me] = ybuf[me]
 
     wait_all(out_ref, out_sem)
+    pltpu.make_async_copy(whole, whole, part_send).wait()
     wait_all(hbuf, tap_out)
     wait_all(xbuf, sig_out)
     wait_all(ybuf, out_out)
 
 
-def exchange(sig, taps):
-    n, cpd, rows = sig.shape
+def exchange(signal, filters):
+    n, m = lax.axis_size("seq"), lax.axis_size("ch")
+    rows, width = signal.shape
+    cpd = width // n
     total, pad = n * cpd, 6 * cpd
     blocks = n * rows // LANES + 1
+    groups = filters.shape[1] // m
     vmem = pl.BlockSpec(memory_space=pltpu.VMEM)
     return pl.pallas_call(
-        functools.partial(exchange_kernel, n),
-        out_shape=jax.ShapeDtypeStruct(sig.shape, F32),
+        functools.partial(exchange_kernel, n, m),
+        out_shape=jax.ShapeDtypeStruct((n, cpd, rows), F32),
         in_specs=[vmem, vmem],
         out_specs=vmem,
         scratch_shapes=[
-            pltpu.VMEM(sig.shape, F32),
+            pltpu.VMEM((n, cpd, rows), F32),
+            pltpu.VMEM((m, groups, LANES), F32),
+            pltpu.VMEM((m, groups, LANES), F32),
+            pltpu.VMEM((groups, 1, rows), F32),
+            pltpu.VMEM((n, cpd, rows), F32),
             pltpu.VMEM((n + 1, 1, rows), F32),
-            pltpu.VMEM(sig.shape, F32),
+            pltpu.VMEM((n, cpd, rows), F32),
             pltpu.VMEM((pad + total, 2 * rows), BF),
             pltpu.VMEM((pad + total, 2 * rows), BF),
             pltpu.VMEM((blocks, LANES, LANES), BF),
             pltpu.VMEM((blocks, LANES, LANES), BF),
-            *[pltpu.SemaphoreType.DMA] * 6,
+            *[pltpu.SemaphoreType.DMA] * 8,
         ],
         compiler_params=pltpu.CompilerParams(
             collective_id=0, has_side_effects=True, vmem_limit_bytes=48 * 1024 * 1024
         ),
-    )(sig, taps)
+    )(signal, filters)
 
 
 def body(signal, filters, skip_gain):
-    n = lax.axis_size("seq")
     rows, width = signal.shape
-    taps = lax.all_to_all(filters, "ch", split_axis=1, concat_axis=0, tiled=True)
-    groups = taps.shape[1]
-    taps = taps.T.reshape(groups, 1, rows)
-    sig = signal.T.reshape(n, width // n, rows)
-    values = exchange(sig, taps)
+    values = exchange(signal, filters)
     return values.reshape(width, rows).T + skip_gain[None, :] * signal
 
 

time: 99.3 us -> 82 us (0.83)
  starting transfers between devices: 10.1 us -> 0 us
  waiting for transfers between devices: 3.49 us -> 0 us
  local copies, waits for them, and re-layouts: 4.66 us -> 2.82 us
  Pallas kernels: 79 us -> 78 us
    all_to_all x1 -> x0, starting transfers between devices: 10.1 us -> none  [body(): lax.all_to_all(filters, 'ch', split_axis=1, concat_axis=0, tiled=True)]
    all_to_all x1 -> x0, waiting for transfers between devices: 3.49 us -> none  [body(): lax.all_to_all(filters, 'ch', split_axis=1, concat_axis=0, tiled=True)]
    transpose x1 -> x0, local copies, waits for them, and re-layouts: 1.24 us -> none  [body(): sig = signal.T.reshape(n, width // n, rows)]
    pallas_call x1, Pallas kernels: 79 us -> 78 us  [exchange(): pl.pallas_call(functools.partial(exchange_kernel, n, m), out_shape=jax.Sh...]
    unnamed x7 -> x8, local copies, waits for them, and re-layouts: 2.51 us -> 2.63 us
  transfers between devices with their start and end apart: 1 -> 0, of which waited for: 1 -> 0; matrix products, arithmetic and copies ran while one was open for 1% -> 0% of each run, Pallas kernels for 0% -> 0%
where the time goes in v2:
time: 82 us; the launch traced here: 81.7 us
  Pallas kernels  78 us (95%)
  local copies, waits for them, and re-layouts  2.82 us (3%)
  other arithmetic  0.89 us (1%)
    pallas_call x1, Pallas kernels, exchange(): pl.pallas_call(functools.partial(exchange_kernel, n, m), out_shape=jax.Sh...  78 us
    unnamed x8, local copies, waits for them, and re-layouts  2.63 us

profile of v2, /device:TPU:1, one launch (start us, length us, event | category | flops | bytes accessed | tf_op | source)
XLA Modules:
  0.0 81.7 jit_solution(9838785509788040968)
XLA Ops:
  0.0 0.0 copy-start
  0.0 1.0 %copy-done = f32[256,512]{1,0:T(8,128)S(1)} copy-done((f32[256,512]{1,0:T(8,128)S(1)}, f32[256,512]{1,0:T(8,128)}, u32[]{:S(2)}) %copy-start) | copy-done | bytes 524312
  1.0 0.0 copy-start.2
  1.0 0.8 copy-done.2
  1.8 78.0 %shard_map.37 = f32[64,8,256]{2,1,0:T(8,128)S(1)} custom-call(f32[256,512]{1,0:T(8,128)S(1)} %copy-done, f32[32,256]{1,0:T(8,128)S(1)} %copy-done.2), custom_call_target="tpu_custom_call" | custom-call | tf_op jit(solution)/shard_map/pallas_call | solution.py:222
  79.8 0.0 copy-start.1
  79.8 0.0 copy-start.3
  79.8 0.2 copy.4
  80.0 0.8 copy-done.1
  80.8 0.0 copy-done.3
  80.8 0.9 %bitcast_add_fusion = f32[256,512]{1,0:T(8,128)} fusion(f32[512,256]{0,1:T(8,128)S(1)} %copy.4, f32[256,512]{1,0:T(8,128)S(1)} %copy-done.1, f32[512]{0:T(512)S(1)} %copy-done.3), kind=kLoop, calls=%fused_computation | loop fusion | flops 262144 | bytes 1574912 | tf_op jit(solution)/shard_map/add | solution.py:250
Async XLA Ops:
  0.0 1.0 %copy-start = (f32[256,512]{1,0:T(8,128)S(1)}, f32[256,512]{1,0:T(8,128)}, u32[]{:S(2)}) copy-start(f32[256,512]{1,0:T(8,128)} %sig_in.1) | copy-start | bytes 1572868
  1.0 0.8 copy-start.2
  79.8 1.0 %copy-start.1 = (f32[256,512]{1,0:T(8,128)S(1)}, f32[256,512]{1,0:T(8,128)}, u32[]{:S(2)}) copy-start(f32[256,512]{1,0:T(8,128)} %sig_in.1) | copy-start | bytes 1572868
  79.8 1.0 %copy-start.3 = (f32[512]{0:T(512)S(1)}, f32[512]{0:T(512)}, u32[]{:S(2)}) copy-start(f32[512]{0:T(512)} %param.5) | copy-start | bytes 6148

commit v3 on v2

v3 whole, which is shorter than its diff:
```python
import functools

import jax
import jax.numpy as jnp
from jax import lax
from jax.experimental import pallas as pl
from jax.experimental.pallas import tpu as pltpu
from jax.sharding import PartitionSpec as P

GROUP = 16
LANES = 128
MESH = pl.DeviceIdType.MESH
BF = jnp.bfloat16
F32 = jnp.float32


def split(value):
    high = value.astype(BF)
    return high, (value - high.astype(F32)).astype(BF)


def swap(left, right):
    half = left.shape[1] // 2
    first = lax.broadcasted_iota(jnp.int32, left.shape, 1) < half
    return (
        jnp.where(first, left, pltpu.roll(right, half, 1)),
        jnp.where(first, pltpu.roll(left, half, 1), right),
    )


def exchange_kernel(
    n, m, sig_in, tap_in, out_ref, sig_ref, part_out, part_in, tap_ref, xbuf, hbuf, ybuf, landed, xx_hi, xx_lo,
    ysum, strip_hi, strip_lo, part_send, tap_out, part_sem, tap_sem, sig_out, out_out, sig_sem, out_sem,
):
    me = lax.axis_index("seq")
    mine = lax.axis_index("ch")
    cpd, rows = sig_ref.shape[2], 2 * LANES
    per = rows // LANES
    barrier = pltpu.get_barrier_semaphore()

    def peer(step):
        away = n // 2 - step // 2
        return lax.rem(me + jnp.where(step % 2 == 1, away, n - away), n)

    @pl.loop(1, n)
    def _(step):
        pl.semaphore_signal(barrier, inc=1, device_id={"seq": peer(step)}, device_id_type=MESH)

    @pl.loop(1, m)
    def _(step):
        pl.semaphore_signal(barrier, inc=1, device_id={"ch": lax.rem(mine + step, m)}, device_id_type=MESH)

    lags = tap_in.shape[0]
    slots = LANES // lags
    tiled = jnp.concatenate([tap_in[...]] * slots, axis=0).T
    lane = lax.broadcasted_iota(jnp.int32, tiled.shape, 1)
    start = lags * lax.rem(mine, slots)
    tiled = jnp.where((lane >= start) & (lane < start + lags), tiled, 0.0)
    part_out[...] = tiled.reshape(part_out.shape)

    for first in range(0, n * cpd, LANES):
        turned = sig_in[:, first:first + LANES].T
        turned = turned.reshape(LANES // cpd, cpd, rows)
        for half, value in enumerate(swap(turned[:, :, :LANES], turned[:, :, LANES:])):
            sig_ref[half, first // cpd:(first + LANES) // cpd] = value

    pl.semaphore_wait(barrier, n + m - 2)

    def part_copy(step):
        other = lax.rem(mine + step, m)
        return pltpu.make_async_remote_copy(
            src_ref=part_out.at[other], dst_ref=part_in.at[mine], send_sem=part_send,
            recv_sem=part_sem, device_id={"ch": other}, device_id_type=MESH,
        )

    def tap_copy(step):
        other = peer(step)
        return pltpu.make_async_remote_copy(
            src_ref=tap_ref.at[other // 2], dst_ref=hbuf.at[me + 1], send_sem=tap_out,
            recv_sem=tap_sem, device_id={"seq": other}, device_id_type=MESH,
        )

    def sig_copy(step, half):
        other = peer(step)
        return pltpu.make_async_remote_copy(
            src_ref=sig_ref.at[half, other], dst_ref=xbuf.at[half, me], send_sem=sig_out.at[half],
            recv_sem=sig_sem.at[half], device_id={"seq": other}, device_id_type=MESH,
        )

    def out_copy(other, half):
        return pltpu.make_async_remote_copy(
            src_ref=ybuf.at[half, other], dst_ref=landed.at[half, me], send_sem=out_out.at[half],
            recv_sem=out_sem.at[half], device_id={"seq": other}, device_id_type=MESH,
        )

    @pl.loop(1, m)
    def _(step):
        part_copy(step).start()

    ahead = n // 4

    @pl.loop(1, ahead)
    def _(step):
        sig_copy(step, 0).start()

    part_in[mine] = part_out[mine]
    whole = part_in.at[pl.ds(0, m - 1)]
    pltpu.make_async_copy(whole, whole, part_sem).wait()
    for half in range(m // slots):
        value = part_in[half * slots]
        for slot in range(1, slots):
            value = value + part_in[half * slots + slot]
        for group in range(n // 2):
            tap_ref[group, :, half * LANES:(half + 1) * LANES] = value[group:group + 1]

    @pl.loop(ahead, ahead + 4)
    def _(step):
        sig_copy(step, 0).start()

    @pl.loop(1, n)
    def _(step):
        tap_copy(step).start()

    @pl.loop(ahead + 4, n)
    def _(step):
        sig_copy(step, 0).start()

    @pl.loop(1, n)
    def _(step):
        sig_copy(step, 1).start()

    hbuf[0] = jnp.zeros((1, rows), F32)
    hbuf[me + 1] = tap_ref[me // 2]
    for half in range(2):
        xbuf[half, me] = sig_ref[half, me]

    def wait_all(ref, sem):
        whole = ref.at[pl.ds(0, n - 1)]
        pltpu.make_async_copy(whole, whole, sem).wait()

    wait_all(hbuf, tap_sem)

    strip_hi[0] = jnp.zeros((LANES, LANES), BF)
    strip_lo[0] = jnp.zeros((LANES, LANES), BF)

    def build(pair, block):
        spread = jnp.broadcast_to(pair, (LANES, 2 * LANES))
        rolled = pltpu.roll(spread, 0, 1, stride=1, stride_axis=0)[:, LANES:]
        high, low = split(rolled)
        strip_hi[block] = high
        strip_lo[block] = low

    @pl.loop(0, n)
    def _(source):
        before = hbuf[source, :, rows - LANES:]
        build(jnp.concatenate([before, hbuf[source + 1, :, :LANES]], axis=1), source * per + 1)
        for part in range(1, per):
            pair = hbuf[source + 1, :, (part - 1) * LANES:(part + 1) * LANES]
            build(pair, source * per + part + 1)

    deep = cpd // 2
    total = n * deep
    depth = xx_hi.shape[1] // rows

    def toeplitz(strip, step):
        first = step * depth * per

        def line(start):
            return jnp.concatenate([strip[start + part] for part in range(per)], axis=1)

        lines = []
        for lag in range(depth):
            for part in range(per):
                lines.append(line(first + lag * per + 1 - part))
        return jnp.concatenate(lines, axis=0)

    @pl.loop(0, 2)
    def _(half):
        wait_all(xbuf.at[half], sig_sem.at[half])

        pairs = xbuf[half].reshape(n // 2, 2 * cpd, LANES)
        sides = swap(pairs[:, :cpd], pairs[:, cpd:])
        value = jnp.concatenate([side.reshape(total, LANES) for side in sides], axis=1)
        row = lax.broadcasted_iota(jnp.int32, value.shape, 0)
        for lag in range(depth):
            shifted = value
            if lag > 0:
                shifted = jnp.where(row < lag * deep, 0.0, pltpu.roll(value, lag * deep, 0))
            high, low = split(shifted)
            xx_hi[:, lag * rows:(lag + 1) * rows] = high
            xx_lo[:, lag * rows:(lag + 1) * rows] = low

        for step in range(n // depth):
            base = step * depth * deep
            height = total - base
            weight_hi, weight_lo = toeplitz(strip_hi, step), toeplitz(strip_lo, step)
            lhs_hi, lhs_lo = xx_hi[:height], xx_lo[:height]
            dot = functools.partial(jnp.dot, preferred_element_type=F32)
            value = dot(lhs_hi, weight_hi) + dot(lhs_lo, weight_hi) + dot(lhs_hi, weight_lo)
            if step > 0:
                value = value + ysum[base:]
            ysum[base:] = value
            done = value[:depth * deep].reshape(depth // 2, cpd, rows)
            for odd, side in enumerate(swap(done[:, :, :LANES], done[:, :, LANES:])):
                for pair in range(depth // 2):
                    ybuf[half, step * depth + 2 * pair + odd] = side[pair]

            @pl.loop(step * depth, (step + 1) * depth)
            def _(other):
                @pl.when(other != me)
                def _():
                    out_copy(other, half).start()

    for half in range(2):
        landed[half, me] = ybuf[half, me]
        wait_all(landed.at[half], out_sem.at[half])
    for side, value in enumerate(swap(landed[0], landed[1])):
        out_ref[:, :, side * LANES:(side + 1) * LANES] = value

    pltpu.make_async_copy(whole, whole, part_send).wait()
    wait_all(hbuf, tap_out)
    for half in range(2):
        wait_all(xbuf.at[half], sig_out.at[half])
        wait_all(ybuf.at[half], out_out.at[half])


def exchange(signal, filters):
    n, m = lax.axis_size("seq"), lax.axis_size("ch")
    rows, width = signal.shape
    cpd = width // n
    total, depth = n * cpd // 2, 4
    message = (2, n, cpd, LANES)
    blocks = n * rows // LANES + 1
    groups = filters.shape[1] // m
    vmem = pl.BlockSpec(memory_space=pltpu.VMEM)
    return pl.pallas_call(
        functools.partial(exchange_kernel, n, m),
        out_shape=jax.ShapeDtypeStruct((n, cpd, rows), F32),
        in_specs=[vmem, vmem],
        out_specs=vmem,
        scratch_shapes=[
            pltpu.VMEM(message, F32),
            pltpu.VMEM((m, groups, LANES), F32),
            pltpu.VMEM((m, groups, LANES), F32),
            pltpu.VMEM((groups, 1, rows), F32),
            pltpu.VMEM(message, F32),
            pltpu.VMEM((n + 1, 1, rows), F32),
            pltpu.VMEM(message, F32),
            pltpu.VMEM(message, F32),
            pltpu.VMEM((total, depth * rows), BF),
            pltpu.VMEM((total, depth * rows), BF),
            pltpu.VMEM((total, rows), F32),
            pltpu.VMEM((blocks, LANES, LANES), BF),
            pltpu.VMEM((blocks, LANES, LANES), BF),
            *[pltpu.SemaphoreType.DMA] * 4,
            *[pltpu.SemaphoreType.DMA((2,))] * 4,
        ],
        compiler_params=pltpu.CompilerParams(
            collective_id=0, has_side_effects=True, vmem_limit_bytes=48 * 1024 * 1024
        ),
    )(signal, filters)


def body(signal, filters, skip_gain):
    rows, width = signal.shape
    values = exchange(signal, filters)
    return values.reshape(width, rows).T + skip_gain[None, :] * signal


def solution(mesh):
    placed = (P("seq", "ch"), P(("seq", "ch"), None), P("ch"))
    return jax.shard_map(
        body, mesh=mesh, in_specs=placed, out_specs=P("seq", "ch"), check_vma=False
    )
```

time: 82 us -> 73.6 us (0.90)
  Pallas kernels: 78 us -> 69.6 us
    pallas_call x1, Pallas kernels: 78 us -> 69.6 us  [exchange(): pl.pallas_call(functools.partial(exchange_kernel, n, m), out_shape=jax.Sh...]
where the time goes in v3:
time: 73.6 us; the launch traced here: 73.3 us
  Pallas kernels  69.6 us (95%)
  local copies, waits for them, and re-layouts  2.82 us (4%)
  other arithmetic  0.89 us (1%)
    pallas_call x1, Pallas kernels, exchange(): pl.pallas_call(functools.partial(exchange_kernel, n, m), out_shape=jax.Sh...  69.6 us
    unnamed x8, local copies, waits for them, and re-layouts  2.63 us

profile of v3, /device:TPU:1, one launch (start us, length us, event | category | flops | bytes accessed | tf_op | source)
XLA Modules:
  0.0 73.3 jit_solution(10930274055076440050)
XLA Ops:
  0.0 0.0 copy-start
  0.0 1.0 %copy-done = f32[256,512]{1,0:T(8,128)S(1)} copy-done((f32[256,512]{1,0:T(8,128)S(1)}, f32[256,512]{1,0:T(8,128)}, u32[]{:S(2)}) %copy-start) | copy-done | bytes 524312
  1.0 0.0 copy-start.2
  1.0 0.8 %copy-done.2 = f32[32,256]{1,0:T(8,128)S(1)} copy-done((f32[32,256]{1,0:T(8,128)S(1)}, f32[32,256]{1,0:T(8,128)}, u32[]{:S(2)}) %copy-start.2) | copy-done | bytes 32792
  1.8 69.6 %shard_map.37 = f32[64,8,256]{2,1,0:T(8,128)S(1)} custom-call(f32[256,512]{1,0:T(8,128)S(1)} %copy-done, f32[32,256]{1,0:T(8,128)S(1)} %copy-done.2), custom_call_target="tpu_custom_call" | custom-call | tf_op jit(solution)/shard_map/pallas_call | solution.py:236
  71.4 0.0 copy-start.1
  71.4 0.0 copy-start.3
  71.4 0.2 copy.4
  71.6 0.8 %copy-done.1 = f32[256,512]{1,0:T(8,128)S(1)} copy-done((f32[256,512]{1,0:T(8,128)S(1)}, f32[256,512]{1,0:T(8,128)}, u32[]{:S(2)}) %copy-start.1) | copy-done | bytes 524312
  72.4 0.0 copy-done.3
  72.5 0.9 %bitcast_add_fusion = f32[256,512]{1,0:T(8,128)} fusion(f32[512,256]{0,1:T(8,128)S(1)} %copy.4, f32[256,512]{1,0:T(8,128)S(1)} %copy-done.1, f32[512]{0:T(512)S(1)} %copy-done.3), kind=kLoop, calls=%fused_computation | loop fusion | flops 262144 | bytes 1574912 | tf_op jit(solution)/shard_map/add | solution.py:267
Async XLA Ops:
  0.0 1.0 %copy-start = (f32[256,512]{1,0:T(8,128)S(1)}, f32[256,512]{1,0:T(8,128)}, u32[]{:S(2)}) copy-start(f32[256,512]{1,0:T(8,128)} %sig_in.1) | copy-start | bytes 1572868
  1.0 0.8 %copy-start.2 = (f32[32,256]{1,0:T(8,128)S(1)}, f32[32,256]{1,0:T(8,128)}, u32[]{:S(2)}) copy-start(f32[32,256]{1,0:T(8,128)} %tap_in.1) | copy-start | bytes 98308
  71.4 1.0 %copy-start.1 = (f32[256,512]{1,0:T(8,128)S(1)}, f32[256,512]{1,0:T(8,128)}, u32[]{:S(2)}) copy-start(f32[256,512]{1,0:T(8,128)} %sig_in.1) | copy-start | bytes 1572868
  71.4 1.0 %copy-start.3 = (f32[512]{0:T(512)S(1)}, f32[512]{0:T(512)}, u32[]{:S(2)}) copy-start(f32[512]{0:T(512)} %param.5) | copy-start | bytes 6148

commit v4 on v3

--- a/solution.py
+++ b/solution.py
@@ -214,8 +214,11 @@
     for half in range(2):
         landed[half, me] = ybuf[half, me]
         wait_all(landed.at[half], out_sem.at[half])
-    for side, value in enumerate(swap(landed[0], landed[1])):
-        out_ref[:, :, side * LANES:(side + 1) * LANES] = value
+    for first in range(0, n * cpd, LANES):
+        peers = slice(first // cpd, (first + LANES) // cpd)
+        sides = swap(landed[0, peers], landed[1, peers])
+        value = jnp.concatenate([side.reshape(LANES, LANES).T for side in sides], axis=0)
+        out_ref[:, first:first + LANES] = value
 
     pltpu.make_async_copy(whole, whole, part_send).wait()
     wait_all(hbuf, tap_out)
@@ -235,7 +238,7 @@
     vmem = pl.BlockSpec(memory_space=pltpu.VMEM)
     return pl.pallas_call(
         functools.partial(exchange_kernel, n, m),
-        out_shape=jax.ShapeDtypeStruct((n, cpd, rows), F32),
+        out_shape=jax.ShapeDtypeStruct(signal.shape, F32),
         in_specs=[vmem, vmem],
         out_specs=vmem,
         scratch_shapes=[
@@ -262,9 +265,7 @@
 
 
 def body(signal, filters, skip_gain):
-    rows, width = signal.shape
-    values = exchange(signal, filters)
-    return values.reshape(width, rows).T + skip_gain[None, :] * signal
+    return exchange(signal, filters) + skip_gain[None, :] * signal
 
 
 def solution(mesh):

time: 73.6 us -> 72.8 us (0.989)
  local copies, waits for them, and re-layouts: 2.82 us -> 1.8 us
    unnamed x8 -> x6, local copies, waits for them, and re-layouts: 2.63 us -> 1.8 us
where the time goes in v4:
time: 72.8 us; the launch traced here: 72.5 us
  Pallas kernels  69.8 us (96%)
  local copies, waits for them, and re-layouts  1.8 us (2%)
  other arithmetic  0.89 us (1%)
    pallas_call x1, Pallas kernels, exchange(): pl.pallas_call(functools.partial(exchange_kernel, n, m), out_shape=jax.Sh...  69.8 us
    unnamed x6, local copies, waits for them, and re-layouts  1.8 us

profile of v4, /device:TPU:1, one launch (start us, length us, event | category | flops | bytes accessed | tf_op | source)
XLA Modules:
  0.0 72.5 jit_solution(13051498261164048083)
XLA Ops:
  0.0 0.0 copy-start
  0.0 1.0 %copy-done = f32[256,512]{1,0:T(8,128)S(1)} copy-done((f32[256,512]{1,0:T(8,128)S(1)}, f32[256,512]{1,0:T(8,128)}, u32[]{:S(2)}) %copy-start) | copy-done | bytes 524312
  1.0 0.0 copy-start.1
  1.0 0.8 %copy-done.1 = f32[32,256]{1,0:T(8,128)S(1)} copy-done((f32[32,256]{1,0:T(8,128)S(1)}, f32[32,256]{1,0:T(8,128)}, u32[]{:S(2)}) %copy-start.1) | copy-done | bytes 32792
  1.8 0.0 copy-start.2
  1.8 69.8 %shard_map.37 = f32[256,512]{1,0:T(8,128)S(1)} custom-call(f32[256,512]{1,0:T(8,128)S(1)} %copy-done, f32[32,256]{1,0:T(8,128)S(1)} %copy-done.1), custom_call_target="tpu_custom_call" | custom-call | tf_op jit(solution)/shard_map/pallas_call | solution.py:239
  71.6 0.0 copy-done.2
  71.6 0.9 %multiply_add_fusion = f32[256,512]{1,0:T(8,128)} fusion(f32[256,512]{1,0:T(8,128)S(1)} %shard_map.37, f32[256,512]{1,0:T(8,128)S(1)} %copy-done, f32[512]{0:T(512)S(1)} %copy-done.2), kind=kLoop, calls=%fused_computation | loop fusion | flops 262144 | bytes 1574912 | tf_op jit(solution)/shard_map/add | solution.py:268
Async XLA Ops:
  0.0 1.0 %copy-start = (f32[256,512]{1,0:T(8,128)S(1)}, f32[256,512]{1,0:T(8,128)}, u32[]{:S(2)}) copy-start(f32[256,512]{1,0:T(8,128)} %sig_in.1) | copy-start | bytes 1572868
  1.0 0.8 %copy-start.1 = (f32[32,256]{1,0:T(8,128)S(1)}, f32[32,256]{1,0:T(8,128)}, u32[]{:S(2)}) copy-start(f32[32,256]{1,0:T(8,128)} %tap_in.1) | copy-start | bytes 98308
  1.8 69.8 %copy-start.2 = (f32[512]{0:T(512)S(1)}, f32[512]{0:T(512)}, u32[]{:S(2)}) copy-start(f32[512]{0:T(512)} %param.5) | copy-start | bytes 6148

commit v5 on v4

--- a/solution.py
+++ b/solution.py
@@ -207,9 +207,15 @@
 
             @pl.loop(step * depth, (step + 1) * depth)
             def _(other):
-                @pl.when(other != me)
+                @pl.when((other != me) & (half == 0))
                 def _():
                     out_copy(other, half).start()
+
+        @pl.when(half == 1)
+        def _():
+            @pl.loop(1, n)
+            def _(step):
+                out_copy(peer(step), half).start()
 
     for half in range(2):
         landed[half, me] = ybuf[half, me]

time: 72.8 us -> 79.4 us (1.091)
  Pallas kernels: 69.8 us -> 76.5 us
    pallas_call x1, Pallas kernels: 69.8 us -> 76.5 us  [exchange(): pl.pallas_call(functools.partial(exchange_kernel, n, m), out_shape=jax.Sh...]
where the time goes in v5:
time: 79.4 us; the launch traced here: 79.2 us
  Pallas kernels  76.5 us (96%)
  local copies, waits for them, and re-layouts  1.8 us (2%)
  other arithmetic  0.89 us (1%)
    pallas_call x1, Pallas kernels, exchange(): pl.pallas_call(functools.partial(exchange_kernel, n, m), out_shape=jax.Sh...  76.5 us
    unnamed x6, local copies, waits for them, and re-layouts  1.8 us

profile of v5, /device:TPU:1, one launch (start us, length us, event | category | flops | bytes accessed | tf_op | source)
XLA Modules:
  0.0 79.2 jit_solution(7285226053619351446)
XLA Ops:
  0.0 0.0 copy-start
  0.0 1.0 %copy-done = f32[256,512]{1,0:T(8,128)S(1)} copy-done((f32[256,512]{1,0:T(8,128)S(1)}, f32[256,512]{1,0:T(8,128)}, u32[]{:S(2)}) %copy-start) | copy-done | bytes 524312
  1.0 0.0 copy-start.1
  1.0 0.8 copy-done.1
  1.8 0.0 copy-start.2
  1.8 76.5 %shard_map.37 = f32[256,512]{1,0:T(8,128)S(1)} custom-call(f32[256,512]{1,0:T(8,128)S(1)} %copy-done, f32[32,256]{1,0:T(8,128)S(1)} %copy-done.1), custom_call_target="tpu_custom_call" | custom-call | tf_op jit(solution)/shard_map/pallas_call | solution.py:245
  78.3 0.0 copy-done.2
  78.3 0.9 %multiply_add_fusion = f32[256,512]{1,0:T(8,128)} fusion(f32[256,512]{1,0:T(8,128)S(1)} %shard_map.37, f32[256,512]{1,0:T(8,128)S(1)} %copy-done, f32[512]{0:T(512)S(1)} %copy-done.2), kind=kLoop, calls=%fused_computation | loop fusion | flops 262144 | bytes 1574912 | tf_op jit(solution)/shard_map/add | solution.py:274
Async XLA Ops:
  0.0 1.0 %copy-start = (f32[256,512]{1,0:T(8,128)S(1)}, f32[256,512]{1,0:T(8,128)}, u32[]{:S(2)}) copy-start(f32[256,512]{1,0:T(8,128)} %sig_in.1) | copy-start | bytes 1572868
  1.0 0.8 copy-start.1
  1.8 76.5 %copy-start.2 = (f32[512]{0:T(512)S(1)}, f32[512]{0:T(512)}, u32[]{:S(2)}) copy-start(f32[512]{0:T(512)} %param.5) | copy-start | bytes 6148
